TPU v7x, 32 devices: a whole 2x2x4 slice. The times are simulated.
32 devices in a mesh: row: 16 (over z, y, x), col: 2 (over core).
Axes of the slice: x: 2, y: 2, z: 4, core: 2. Of those that a mesh axis runs over, the one named last changes fastest.
Arguments:
- samples: bfloat16 [32768, 8192], P('row', 'col'), may hold values from -0.046875 to 0.046875
- targets: float32 [32768, 128], P('row'), may hold values from -6 to 6
- factor_inv: float32 [2, 4096, 4096], P('col', None, 'row'), may hold values from -1 to 1, as said below
Outputs:
- solution: float32 [8192, 128], P('col')
- residual: float32 [32768, 128], P('row')
Inputs may be any that keep to these rules, and one draw needn't show every extreme that they name: Each factor_inv[j] is lower triangular with a positive diagonal.
All inputs are finite; a program needn't handle non-finite values.
Results may differ from a plain program's by a relative error of at most 0.0039.
Values sent between devices are 32-bit elements; how exact they have to be, the bound alone decides.
A program may use at most 128 MiB of HBM per device.

v0:
```python
import jax
import jax.numpy as jnp
from jax import lax
from jax.sharding import PartitionSpec as P

ROUNDS = 3
ridge_weight = 0.5


def run_group(samples, residual, inverse, own_rows, offset, relaxation):
    solution = jnp.zeros((samples.shape[1], residual.shape[1]), jnp.float32)
    for sweep in range(ROUNDS):
        res16 = residual.astype(jnp.bfloat16)
        part_grad = jnp.einsum("rb,rk->bk", samples, res16, preferred_element_type=jnp.float32)
        own_solution = lax.dynamic_slice_in_dim(solution, offset, own_rows, 0)
        grad_own = (
            lax.psum_scatter(part_grad, "row", scatter_dimension=0, tiled=True)
            - ridge_weight * own_solution
        )
        term = jnp.dot(inverse, grad_own, precision=lax.Precision.HIGHEST)
        image = lax.psum(term, "row")
        update_own = jnp.einsum("bc,bk->ck", inverse, image, precision=lax.Precision.HIGHEST)
        update = lax.all_gather(update_own, "row", axis=0, tiled=True)
        solution = solution + relaxation * update
        change = jnp.dot(samples, update.astype(jnp.bfloat16), preferred_element_type=jnp.float32)
        residual = residual - relaxation * lax.psum(change, "col")
    return (solution, residual)


def per_device(samples, targets, factor_inv):
    inverse = factor_inv[0]
    own_rows = inverse.shape[1]
    offset = lax.axis_index("row") * own_rows
    relaxation = 1.0 / lax.axis_size("col")
    solution, residual = run_group(samples, targets, inverse, own_rows, offset, relaxation)
    return (solution, residual)


def solution(mesh):
    in_specs = (P("row", "col"), P("row", None), P("col", None, "row"))
    out_specs = (P("col", None), P("row", None))
    return jax.shard_map(
        per_device, mesh=mesh, in_specs=in_specs, out_specs=out_specs, check_vma=False
    )
```

profile of v0, /device:TPU:0, one launch (start us, length us, event | category | flops | bytes accessed | tf_op | source)
XLA Modules:
  0.0 985.5 jit_solution(3133331421541427131)
XLA Ops:
  7.2 0.0 reduce-scatter.4.cloned.1.call-start
  7.2 11.9 %fusion.23 = f32[4096,128]{1,0:T(8,128)} fusion(bf16[2048,4096]{1,0:T(8,128)(2,1)} %param.3, f32[2048,128]{1,0:T(8,128)} %param.4), kind=kOutput, calls=%fused_computation.31 | convolution fusion | flops 2147745792 | bytes 19922944 | tf_op jit(solution)/shard_map/rb,rk->bk/dot_general | solution.py:14
  19.1 0.0 all-reduce.7.cloned.1.call-start
  19.2 83.5 %reduce-scatter.4.cloned.1.call-done = f32[256,128]{1,0:T(8,128)} async-done(((f32[4096,128]{1,0:T(8,128)}), f32[256,128]{1,0:T(8,128)}) %reduce-scatter.4.cloned.1.call-update) | async-done | bytes 131088 | tf_op jit(solution)/shard_map/reduce_scatter | solution.py:17
  102.7 8.1 convolution_bitcast_fusion.4
  110.7 0.0 all-reduce.7.cloned.1.call-update
  110.8 0.0 all-gather.4.cloned.1.call-start
  110.8 123.0 %all-reduce.7.cloned.1.call-done = f32[4096,128]{0,1:T(8,128)} async-done(((f32[4096,128]{0,1:T(8,128)}), f32[4096,128]{0,1:T(8,128)}) %all-reduce.7.cloned.1.call-update) | async-done | bytes 2097168 | tf_op jit(solution)/shard_map/psum | solution.py:21
  233.9 5.6 fusion.9
  239.4 0.0 all-gather.4.cloned.1.call-update
  239.5 0.5 all-reduce.9.cloned.1.call-start
  240.0 60.7 %all-gather.4.cloned.1.call-done = f32[4096,128]{0,1:T(8,128)} async-done(((f32[256,128]{0,1:T(8,128)}), f32[4096,128]{0,1:T(8,128)}) %all-gather.4.cloned.1.call-update) | async-done | bytes 2097168 | tf_op jit(solution)/shard_map/all_gather | solution.py:23
  300.7 13.0 %convolution_bitcast_fusion.7 = f32[2048,128]{0,1:T(8,128)} fusion(bf16[2048,4096]{1,0:T(8,128)(2,1)} %param.3, f32[4096,128]{0,1:T(8,128)} %all-gather.4.cloned.1.call-done), kind=kOutput, calls=%fused_computation.16 | convolution fusion | flops 2148007936 | bytes 19922944 | tf_op jit(solution)/shard_map/dot_general | solution.py:25
  313.7 0.0 all-reduce.9.cloned.1.call-update
  313.8 0.0 reduce-scatter.6.cloned.1.call-start
  313.8 0.3 copy.5
  314.2 17.5 %all-reduce.9.cloned.1.call-done = f32[2048,128]{0,1:T(8,128)} async-done(((f32[2048,128]{0,1:T(8,128)}), f32[2048,128]{0,1:T(8,128)}) %all-reduce.9.cloned.1.call-update) | async-done | bytes 1048592 | tf_op jit(solution)/shard_map/psum | solution.py:26
  331.7 9.8 convolution_bitcast_fusion.1
  341.5 0.0 all-reduce.11.cloned.1.call-start
  341.6 1.5 copy-done
  343.1 1.5 broadcast_multiply_fusion
  344.6 78.9 %reduce-scatter.6.cloned.1.call-done = f32[256,128]{0,1:T(8,128)} async-done(((f32[4096,128]{0,1:T(8,128)}), f32[256,128]{0,1:T(8,128)}) %reduce-scatter.6.cloned.1.call-update) | async-done | bytes 131088 | tf_op jit(solution)/shard_map/reduce_scatter | solution.py:17
  423.5 7.9 convolution_bitcast_fusion.3
  431.4 0.0 all-reduce.11.cloned.1.call-update
  431.4 0.2 all-gather.6.cloned.1.call-start
  431.6 122.8 %all-reduce.11.cloned.1.call-done = f32[4096,128]{0,1:T(8,128)} async-done(((f32[4096,128]{0,1:T(8,128)}), f32[4096,128]{0,1:T(8,128)}) %all-reduce.11.cloned.1.call-update) | async-done | bytes 2097168 | tf_op jit(solution)/shard_map/psum | solution.py:21
  554.5 5.6 fusion.12
  560.1 0.0 all-reduce.13.cloned.1.call-start
  560.1 61.2 %all-gather.6.cloned.1.call-done = f32[4096,128]{0,1:T(8,128)} async-done(((f32[256,128]{0,1:T(8,128)}), f32[4096,128]{0,1:T(8,128)}) %all-gather.6.cloned.1.call-update) | async-done | bytes 2097168 | tf_op jit(solution)/shard_map/all_gather | solution.py:23
  621.3 13.0 %convolution_bitcast_fusion.6 = f32[2048,128]{0,1:T(8,128)} fusion(bf16[2048,4096]{1,0:T(8,128)(2,1)} %param.3, f32[4096,128]{0,1:T(8,128)} %all-gather.6.cloned.1.call-done), kind=kOutput, calls=%fused_computation.15 | convolution fusion | flops 2148007936 | bytes 19922944 | tf_op jit(solution)/shard_map/dot_general | solution.py:25
  634.4 0.0 reduce-scatter.8.cloned.1.call-start
  634.4 17.9 %all-reduce.13.cloned.1.call-done = f32[2048,128]{0,1:T(8,128)} async-done(((f32[2048,128]{0,1:T(8,128)}), f32[2048,128]{0,1:T(8,128)}) %all-reduce.13.cloned.1.call-update) | async-done | bytes 1048592 | tf_op jit(solution)/shard_map/psum | solution.py:26
  652.3 10.2 %convolution_bitcast_fusion = f32[4096,128]{0,1:T(8,128)} fusion(bf16[2048,4096]{1,0:T(8,128)(2,1)} %param.3, f32[2048,128]{0,1:T(8,128)} %all-reduce.13.cloned.1.call-done, f32[2048,128]{0,1:T(8,128)S(1)} %copy.5, f32[2048,128]{0,1:T(8,128)} %all-reduce.9.cloned.1.call-done), kind=kOutput, calls=%fused_computation | convolution fusion | flops 2148794368 | bytes 22020096 | tf_op jit(solution)/shard_map/rb,rk->bk/dot_general | solution.py:14
  662.5 0.3 all-reduce.15.cloned.1.call-start
  662.8 3.2 multiply_add_fusion.1
  665.9 78.6 %reduce-scatter.8.cloned.1.call-done = f32[256,128]{0,1:T(8,128)} async-done(((f32[4096,128]{0,1:T(8,128)}), f32[256,128]{0,1:T(8,128)}) %reduce-scatter.8.cloned.1.call-update) | async-done | bytes 131088 | tf_op jit(solution)/shard_map/reduce_scatter | solution.py:17
  744.5 7.9 convolution_bitcast_fusion.2
  752.5 0.0 all-gather.8.cloned.1.call-start
  752.6 122.8 %all-reduce.15.cloned.1.call-done = f32[4096,128]{0,1:T(8,128)} async-done(((f32[4096,128]{0,1:T(8,128)}), f32[4096,128]{0,1:T(8,128)}) %all-reduce.15.cloned.1.call-update) | async-done | bytes 2097168 | tf_op jit(solution)/shard_map/psum | solution.py:21
  875.4 5.6 fusion.15
  881.0 0.0 all-reduce.17.cloned.1.call-start
  881.0 61.2 %all-gather.8.cloned.1.call-done = f32[4096,128]{0,1:T(8,128)} async-done(((f32[256,128]{0,1:T(8,128)}), f32[4096,128]{0,1:T(8,128)}) %all-gather.8.cloned.1.call-update) | async-done | bytes 2097168 | tf_op jit(solution)/shard_map/all_gather | solution.py:23
  942.2 13.2 %convolution_bitcast_fusion.5 = f32[2048,128]{0,1:T(8,128)} fusion(bf16[2048,4096]{1,0:T(8,128)(2,1)} %param.3, f32[4096,128]{0,1:T(8,128)} %all-gather.8.cloned.1.call-done), kind=kOutput, calls=%fused_computation.14 | convolution fusion | flops 2148007936 | bytes 19922944 | tf_op jit(solution)/shard_map/dot_general | solution.py:25
  955.4 3.1 multiply_add_fusion
  958.6 3.3 copy.6
  961.9 11.5 %all-reduce.17.cloned.1.call-done = f32[2048,128]{0,1:T(8,128)} async-done(((f32[2048,128]{0,1:T(8,128)}), f32[2048,128]{0,1:T(8,128)}) %all-reduce.17.cloned.1.call-update) | async-done | bytes 1048592 | tf_op jit(solution)/shard_map/psum | solution.py:26
  973.4 2.5 multiply_subtract_fusion
  975.9 2.5 copy.7
  (17 shorter events, 0.1 us)
Async XLA Ops:
  7.2 95.5 %reduce-scatter.4.cloned.1.call-start = ((), (), s32[]{:S(2)}) async-start(), calls=%async_computation.3 | async-start | bytes 2228224 | tf_op jit(solution)/shard_map/reduce_scatter | solution.py:17
  19.1 214.7 %all-reduce.7.cloned.1.call-start = ((), (), s32[]{:S(2)}) async-start(), calls=%async_computation.4 | async-start | bytes 4194304 | tf_op jit(solution)/shard_map/psum | solution.py:21
  110.8 190.0 %all-gather.4.cloned.1.call-start = ((), (), s32[]{:S(2)}) async-start(), calls=%async_computation.5 | async-start | bytes 2228224 | tf_op jit(solution)/shard_map/all_gather | solution.py:23
  239.5 74.4 %copy-start.4 = (f32[2048,128]{1,0:T(8,128)S(1)}, f32[2048,128]{1,0:T(8,128)}, u32[]{:S(2)}) copy-start(f32[2048,128]{1,0:T(8,128)} %param.4) | copy-start | bytes 3145732
  239.5 92.2 %all-reduce.9.cloned.1.call-start = ((), (), s32[]{:S(2)}) async-start(), calls=%async_computation.6 | async-start | bytes 2097152 | tf_op jit(solution)/shard_map/psum | solution.py:26
  313.8 109.7 %reduce-scatter.6.cloned.1.call-start = ((), (), s32[]{:S(2)}) async-start(), calls=%async_computation.7 | async-start | bytes 2228224 | tf_op jit(solution)/shard_map/reduce_scatter | solution.py:17
  341.5 1.6 copy-start
  341.5 213.0 %all-reduce.11.cloned.1.call-start = ((), (), s32[]{:S(2)}) async-start(), calls=%async_computation.8 | async-start | bytes 4194304 | tf_op jit(solution)/shard_map/psum | solution.py:21
  431.4 189.9 %all-gather.6.cloned.1.call-start = ((), (), s32[]{:S(2)}) async-start(), calls=%async_computation.9 | async-start | bytes 2228224 | tf_op jit(solution)/shard_map/all_gather | solution.py:23
  560.1 92.3 %all-reduce.13.cloned.1.call-start = ((), (), s32[]{:S(2)}) async-start(), calls=%async_computation.10 | async-start | bytes 2097152 | tf_op jit(solution)/shard_map/psum | solution.py:26
  634.4 110.2 %reduce-scatter.8.cloned.1.call-start = ((), (), s32[]{:S(2)}) async-start(), calls=%async_computation.11 | async-start | bytes 2228224 | tf_op jit(solution)/shard_map/reduce_scatter | solution.py:17
  662.5 212.9 %all-reduce.15.cloned.1.call-start = ((), (), s32[]{:S(2)}) async-start(), calls=%async_computation.12 | async-start | bytes 4194304 | tf_op jit(solution)/shard_map/psum | solution.py:21
  752.5 189.7 %all-gather.8.cloned.1.call-start = ((), (), s32[]{:S(2)}) async-start(), calls=%async_computation.13 | async-start | bytes 2228224 | tf_op jit(solution)/shard_map/all_gather | solution.py:23
  881.0 92.4 %all-reduce.17.cloned.1.call-start = ((), (), s32[]{:S(2)}) async-start(), calls=%async_computation.14 | async-start | bytes 2097152 | tf_op jit(solution)/shard_map/psum | solution.py:26
  942.2 13.2 %copy-start.2 = (f32[4096,128]{0,1:T(8,128)S(1)}, f32[4096,128]{0,1:T(8,128)}, u32[]{:S(2)}) copy-start(f32[4096,128]{0,1:T(8,128)} %multiply_add_fusion.1) | copy-start | bytes 6291460
  958.6 14.8 %copy-start.1 = (f32[2048,128]{0,1:T(8,128)S(1)}, f32[2048,128]{0,1:T(8,128)}, u32[]{:S(2)}) copy-start(f32[2048,128]{0,1:T(8,128)} %all-reduce.9.cloned.1.call-done) | copy-start | bytes 3145732
  958.6 14.8 %copy-start.3 = (f32[2048,128]{0,1:T(8,128)S(1)}, f32[2048,128]{0,1:T(8,128)}, u32[]{:S(2)}) copy-start(f32[2048,128]{0,1:T(8,128)} %all-reduce.13.cloned.1.call-done) | copy-start | bytes 3145732
Sparse Core Ops, SparseCore 0:
  19.3 83.3 reduce-scatter.3
  110.9 122.9 all-reduce.6
  239.6 61.0 all-gather.3
  313.9 17.7 all-reduce.8
  341.6 81.7 reduce-scatter.5
  431.5 122.8 all-reduce.10
  560.2 61.0 all-gather.5
  634.5 17.7 all-reduce.12
  662.6 81.8 reduce-scatter.7
  752.6 122.7 all-reduce.14
  881.1 61.0 all-gather.7
  955.6 17.7 all-reduce.16
where the time goes:
time: 994 us; the launch traced here: 986 us
  waiting for transfers between devices  840 us (85%)
  matrix products  112 us (11%)
  between operations  14.5 us (1%)
  other arithmetic  10.3 us (1%)
    psum x3, waiting for transfers between devices, run_group(): image = lax.psum(term, 'row')  369 us
    reduce_scatter x3, waiting for transfers between devices, run_group(): lax.psum_scatter(part_grad, 'row', scatter_dimension=0, tiled=True)  241 us
    all_gather x3, waiting for transfers between devices, run_group(): update = lax.all_gather(update_own, 'row', axis=0, tiled=True)  183 us
    psum x3, waiting for transfers between devices, run_group(): residual = residual - relaxation * lax.psum(change, 'col')  46.9 us
    dot_general x3, matrix products, run_group(): jnp.dot(samples, update.astype(jnp.bfloat16), preferred_element_type=jnp....  39.2 us
    dot_general x3, matrix products, run_group(): jnp.einsum('rb,rk->bk', samples, res16, preferred_element_type=jnp.float32)  31.9 us
    dot_general x3, matrix products, run_group(): term = jnp.dot(inverse, grad_own, precision=lax.Precision.HIGHEST)  23.9 us
  transfers between devices with their start and end apart: 12, of which 12 were waited for; matrix products, arithmetic and copies ran while one was open for 1% of the time, Pallas kernels for 0%

commit v1 on v0

--- a/solution.py
+++ b/solution.py
@@ -5,6 +5,27 @@
 
 ROUNDS = 3
 ridge_weight = 0.5
+
+
+def collect(array, axis, dim):
+    size, place, span = (lax.axis_size(axis), lax.axis_index(axis), array.shape[dim])
+    right = [(i, (i + 1) % size) for i in range(size)]
+    behind = [(i, (i - 1) % size) for i in range(size)]
+    result = jnp.zeros((*array.shape[:dim], size * span, *array.shape[dim + 1 :]), array.dtype)
+    result = lax.dynamic_update_slice_in_dim(result, array, place * span, axis=dim)
+    from_left = from_right = array
+    half = size // 2
+    for step in range(1, half + 1):
+        from_left = lax.ppermute(from_left, axis, right)
+        result = lax.dynamic_update_slice_in_dim(
+            result, from_left, (place - step) % size * span, axis=dim
+        )
+        if step < size - half:
+            from_right = lax.ppermute(from_right, axis, behind)
+            result = lax.dynamic_update_slice_in_dim(
+                result, from_right, (place + step) % size * span, axis=dim
+            )
+    return result
 
 
 def run_group(samples, residual, inverse, own_rows, offset, relaxation):
@@ -20,7 +41,7 @@
         term = jnp.dot(inverse, grad_own, precision=lax.Precision.HIGHEST)
         image = lax.psum(term, "row")
         update_own = jnp.einsum("bc,bk->ck", inverse, image, precision=lax.Precision.HIGHEST)
-        update = lax.all_gather(update_own, "row", axis=0, tiled=True)
+        update = collect(update_own, "row", 0)
         solution = solution + relaxation * update
         change = jnp.dot(samples, update.astype(jnp.bfloat16), preferred_element_type=jnp.float32)
         residual = residual - relaxation * lax.psum(change, "col")

time: 994 us -> 1040 us (1.046)
  starting transfers between devices: 1.35 us -> 124 us
  waiting for transfers between devices: 840 us -> 732 us
  local copies, waits for them, and re-layouts: 7.7 us -> 34.4 us
    all_gather x3 -> x0, waiting for transfers between devices: 183 us -> none  [run_group(): update = lax.all_gather(update_own, 'row', axis=0, tiled=True)]
    ppermute x0 -> x45, starting transfers between devices: none -> 123 us  [the longest x21 117 us: collect(): from_right = lax.ppermute(from_right, axis, behind)]
    ppermute x0 -> x45, waiting for transfers between devices: none -> 78.2 us  [the longest x24 77.8 us: collect(): from_left = lax.ppermute(from_left, axis, right)]
    ppermute x0 -> x45, local copies, waits for them, and re-layouts: none -> 18.4 us  [the longest x24 16.6 us: collect(): from_left = lax.ppermute(from_left, axis, right)]
    dynamic_update_slice x0 -> x48, local copies, waits for them, and re-layouts: none -> 11.2 us  [the longest x24 5.63 us: collect(): lax.dynamic_update_slice_in_dim(result, from_left, (place - step) % size...]
  transfers between devices with their start and end apart: 12 -> 54, of which waited for: 12 -> 34; matrix products, arithmetic and copies ran while one was open for 1% -> 4% of each run, Pallas kernels for 0% -> 0%
where the time goes in v1:
time: 1040 us; the launch traced here: 1030 us
  waiting for transfers between devices  732 us (70%)
  starting transfers between devices  124 us (12%)
  matrix products  117 us (11%)
  local copies, waits for them, and re-layouts  34.4 us (3%)
  between operations  15.2 us (1%)
    psum x3, waiting for transfers between devices, run_group(): image = lax.psum(term, 'row')  369 us
    reduce_scatter x3, waiting for transfers between devices, run_group(): lax.psum_scatter(part_grad, 'row', scatter_dimension=0, tiled=True)  243 us
    ppermute x21, starting transfers between devices, collect(): from_right = lax.ppermute(from_right, axis, behind)  117 us
    ppermute x24, waiting for transfers between devices, collect(): from_left = lax.ppermute(from_left, axis, right)  77.8 us
    psum x3, waiting for transfers between devices, run_group(): residual = residual - relaxation * lax.psum(change, 'col')  41.9 us
    dot_general x3, matrix products, run_group(): jnp.einsum('rb,rk->bk', samples, res16, preferred_element_type=jnp.float32)  40.4 us
    dot_general x3, matrix products, run_group(): jnp.dot(samples, update.astype(jnp.bfloat16), preferred_element_type=jnp....  37.8 us
    dot_general x3, matrix products, run_group(): term = jnp.dot(inverse, grad_own, precision=lax.Precision.HIGHEST)  24.3 us
  transfers between devices with their start and end apart: 54, of which 34 were waited for; matrix products, arithmetic and copies ran while one was open for 4% of the time, Pallas kernels for 0%

profile of v1, /device:TPU:0, one launch (start us, length us, event | category | flops | bytes accessed | tf_op | source)
XLA Modules:
  0.0 1032.5 jit_solution(9445597813002956916)
XLA Ops:
  7.2 11.9 %fusion.23 = f32[4096,128]{1,0:T(8,128)} fusion(bf16[2048,4096]{1,0:T(8,128)(2,1)} %param.3, f32[2048,128]{1,0:T(8,128)} %param.4), kind=kOutput, calls=%fused_computation.31 | convolution fusion | flops 2147745792 | bytes 19922944 | tf_op jit(solution)/shard_map/rb,rk->bk/dot_general | solution.py:35
  19.2 83.5 %reduce-scatter.4.cloned.1.call-done = f32[256,128]{1,0:T(8,128)} async-done(((f32[4096,128]{1,0:T(8,128)}), f32[256,128]{1,0:T(8,128)}) %reduce-scatter.4.cloned.1.call-update) | async-done | bytes 131088 | tf_op jit(solution)/shard_map/reduce_scatter | solution.py:38
  102.7 8.1 convolution_bitcast_fusion.4
  110.8 123.0 %all-reduce.7.cloned.1.call-done = f32[4096,128]{0,1:T(8,128)} async-done(((f32[4096,128]{0,1:T(8,128)}), f32[4096,128]{0,1:T(8,128)}) %all-reduce.7.cloned.1.call-update) | async-done | bytes 2097168 | tf_op jit(solution)/shard_map/psum | solution.py:42
  233.9 4.9 fusion.9
  240.4 4.2 collective-permute-start.1
  244.8 3.2 collective-permute-done
  248.3 6.0 collective-permute-start.3
  257.1 6.0 collective-permute-start.5
  265.9 6.0 collective-permute-start.7
  274.7 6.1 collective-permute-start.9
  283.5 6.1 collective-permute-start.11
  292.7 6.2 collective-permute-start.13
  302.4 8.4 collective-permute-done.14
  310.9 12.4 %convolution_bitcast_fusion.7 = f32[2048,128]{0,1:T(8,128)} fusion(bf16[2048,4096]{1,0:T(8,128)(2,1)} %param.3, f32[4096,128]{1,0:T(8,128)S(1)} %constant_dynamic-update-slice_fusion.32), kind=kOutput, calls=%fused_computation.16 | convolution fusion | flops 2148007936 | bytes 19922944 | tf_op jit(solution)/shard_map/dot_general | solution.py:46
  325.0 14.0 %all-reduce.9.cloned.1.call-done = f32[2048,128]{0,1:T(8,128)} async-done(((f32[2048,128]{0,1:T(8,128)}), f32[2048,128]{0,1:T(8,128)}) %all-reduce.9.cloned.1.call-update) | async-done | bytes 1048592 | tf_op jit(solution)/shard_map/psum | solution.py:47
  339.0 14.0 %convolution_bitcast_fusion.1 = f32[4096,128]{1,0:T(8,128)} fusion(bf16[2048,4096]{1,0:T(8,128)(2,1)} %param.3, f32[2048,128]{0,1:T(8,128)S(1)} %copy.21, f32[2048,128]{0,1:T(8,128)} %all-reduce.9.cloned.1.call-done), kind=kOutput, calls=%fused_computation.1 | convolution fusion | flops 2148270080 | bytes 20971520 | tf_op jit(solution)/shard_map/rb,rk->bk/dot_general | solution.py:35
  354.6 80.4 %reduce-scatter.6.cloned.1.call-done = f32[256,128]{1,0:T(8,128)} async-done(((f32[4096,128]{1,0:T(8,128)}), f32[256,128]{1,0:T(8,128)}) %reduce-scatter.6.cloned.1.call-update) | async-done | bytes 131088 | tf_op jit(solution)/shard_map/reduce_scatter | solution.py:38
  435.0 8.1 convolution_bitcast_fusion.3
  443.3 123.1 %all-reduce.11.cloned.1.call-done = f32[4096,128]{0,1:T(8,128)} async-done(((f32[4096,128]{0,1:T(8,128)}), f32[4096,128]{0,1:T(8,128)}) %all-reduce.11.cloned.1.call-update) | async-done | bytes 2097168 | tf_op jit(solution)/shard_map/psum | solution.py:42
  566.4 4.9 fusion.12
  572.9 4.2 collective-permute-start.16
  582.5 5.7 collective-permute-start.18
  592.5 5.7 collective-permute-start.20
  602.4 5.7 collective-permute-start.22
  612.3 5.7 collective-permute-start.24
  622.3 5.7 collective-permute-start.26
  632.3 5.7 collective-permute-start.28
  643.0 7.4 collective-permute-done.29
  652.1 13.0 %convolution_bitcast_fusion.6 = f32[2048,128]{0,1:T(8,128)} fusion(bf16[2048,4096]{1,0:T(8,128)(2,1)} %param.3, f32[4096,128]{1,0:T(8,128)} %constant_dynamic-update-slice_fusion.16), kind=kOutput, calls=%fused_computation.15 | convolution fusion | flops 2148007936 | bytes 19922944 | tf_op jit(solution)/shard_map/dot_general | solution.py:46
  665.4 15.4 %all-reduce.13.cloned.1.call-done = f32[2048,128]{0,1:T(8,128)} async-done(((f32[2048,128]{0,1:T(8,128)}), f32[2048,128]{0,1:T(8,128)}) %all-reduce.13.cloned.1.call-update) | async-done | bytes 1048592 | tf_op jit(solution)/shard_map/psum | solution.py:47
  680.8 14.4 %convolution_bitcast_fusion = f32[4096,128]{1,0:T(8,128)} fusion(bf16[2048,4096]{1,0:T(8,128)(2,1)} %param.3, f32[2048,128]{0,1:T(8,128)} %all-reduce.13.cloned.1.call-done, f32[2048,128]{0,1:T(8,128)S(1)} %copy.21, f32[2048,128]{0,1:T(8,128)} %all-reduce.9.cloned.1.call-done), kind=kOutput, calls=%fused_computation | convolution fusion | flops 2148794368 | bytes 22020096 | tf_op jit(solution)/shard_map/rb,rk->bk/dot_general | solution.py:35
  698.4 78.7 %reduce-scatter.8.cloned.1.call-done = f32[256,128]{1,0:T(8,128)} async-done(((f32[4096,128]{1,0:T(8,128)}), f32[256,128]{1,0:T(8,128)}) %reduce-scatter.8.cloned.1.call-update) | async-done | bytes 131088 | tf_op jit(solution)/shard_map/reduce_scatter | solution.py:38
  777.1 8.2 convolution_bitcast_fusion.2
  785.6 123.0 %all-reduce.15.cloned.1.call-done = f32[4096,128]{0,1:T(8,128)} async-done(((f32[4096,128]{0,1:T(8,128)}), f32[4096,128]{0,1:T(8,128)}) %all-reduce.15.cloned.1.call-update) | async-done | bytes 2097168 | tf_op jit(solution)/shard_map/psum | solution.py:42
  908.6 4.9 fusion.15
  915.1 4.2 collective-permute-start.31
  919.5 3.3 collective-permute-done.30
  924.0 5.7 collective-permute-start.33
  934.1 5.7 collective-permute-start.35
  944.0 5.7 collective-permute-start.37
  954.0 5.7 collective-permute-start.39
  964.0 5.7 collective-permute-start.41
  974.0 5.7 collective-permute-start.43
  979.7 3.4 collective-permute-done.42
  984.3 8.7 collective-permute-done.44
  994.0 12.4 %convolution_bitcast_fusion.5 = f32[2048,128]{0,1:T(8,128)} fusion(bf16[2048,4096]{1,0:T(8,128)(2,1)} %param.3, f32[4096,128]{1,0:T(8,128)S(1)} %constant_dynamic-update-slice_fusion), kind=kOutput, calls=%fused_computation.14 | convolution fusion | flops 2148007936 | bytes 19922944 | tf_op jit(solution)/shard_map/dot_general | solution.py:46
  1009.6 12.5 %all-reduce.17.cloned.1.call-done = f32[2048,128]{0,1:T(8,128)} async-done(((f32[2048,128]{0,1:T(8,128)}), f32[2048,128]{0,1:T(8,128)}) %all-reduce.17.cloned.1.call-update) | async-done | bytes 1048592 | tf_op jit(solution)/shard_map/psum | solution.py:47
  (186 shorter events, 94.9 us)
Async XLA Ops:
  7.2 95.5 %reduce-scatter.4.cloned.1.call-start = ((), (), s32[]{:S(2)}) async-start(), calls=%async_computation.3 | async-start | bytes 2228224 | tf_op jit(solution)/shard_map/reduce_scatter | solution.py:38
  19.2 214.7 %all-reduce.7.cloned.1.call-start = ((), (), s32[]{:S(2)}) async-start(), calls=%async_computation.4 | async-start | bytes 4194304 | tf_op jit(solution)/shard_map/psum | solution.py:42
  110.8 228.2 %all-reduce.9.cloned.1.call-start = ((), (), s32[]{:S(2)}) async-start(), calls=%async_computation.5 | async-start | bytes 2097152 | tf_op jit(solution)/shard_map/psum | solution.py:47
  238.8 9.2 collective-permute-start
  256.9 8.7 collective-permute-start.4
  257.1 8.7 collective-permute-start.5
  274.5 8.7 collective-permute-start.8
  274.7 8.7 collective-permute-start.9
  283.3 8.8 collective-permute-start.10
  283.5 9.1 collective-permute-start.11
  292.2 9.9 collective-permute-start.12
  292.7 9.6 collective-permute-start.13
  323.3 111.6 %reduce-scatter.6.cloned.1.call-start = ((), (), s32[]{:S(2)}) async-start(), calls=%async_computation.6 | async-start | bytes 2228224 | tf_op jit(solution)/shard_map/reduce_scatter | solution.py:38
  353.0 213.4 %all-reduce.11.cloned.1.call-start = ((), (), s32[]{:S(2)}) async-start(), calls=%async_computation.7 | async-start | bytes 4194304 | tf_op jit(solution)/shard_map/psum | solution.py:42
  443.1 237.7 %all-reduce.13.cloned.1.call-start = ((), (), s32[]{:S(2)}) async-start(), calls=%async_computation.8 | async-start | bytes 2097152 | tf_op jit(solution)/shard_map/psum | solution.py:47
  571.3 9.3 collective-permute-start.15
  572.9 9.4 collective-permute-start.16
  581.6 9.0 collective-permute-start.17
  582.5 9.9 collective-permute-start.18
  591.6 8.9 collective-permute-start.19
  592.5 9.8 collective-permute-start.20
  601.6 8.9 collective-permute-start.21
  602.4 9.9 collective-permute-start.22
  611.5 9.0 collective-permute-start.23
  612.3 9.9 collective-permute-start.24
  621.5 9.0 collective-permute-start.25
  622.3 9.9 collective-permute-start.26
  631.5 9.0 collective-permute-start.27
  632.3 9.9 collective-permute-start.28
  641.5 8.9 collective-permute-start.29
  665.2 112.0 %reduce-scatter.8.cloned.1.call-start = ((), (), s32[]{:S(2)}) async-start(), calls=%async_computation.9 | async-start | bytes 2228224 | tf_op jit(solution)/shard_map/reduce_scatter | solution.py:38
  695.2 213.4 %all-reduce.15.cloned.1.call-start = ((), (), s32[]{:S(2)}) async-start(), calls=%async_computation.10 | async-start | bytes 4194304 | tf_op jit(solution)/shard_map/psum | solution.py:42
  785.3 236.8 %all-reduce.17.cloned.1.call-start = ((), (), s32[]{:S(2)}) async-start(), calls=%async_computation.11 | async-start | bytes 2097152 | tf_op jit(solution)/shard_map/psum | solution.py:47
  913.5 9.3 collective-permute-start.30
  915.1 8.8 collective-permute-start.31
  923.8 9.0 collective-permute-start.32
  924.0 9.9 collective-permute-start.33
  933.9 8.9 collective-permute-start.34
  934.1 9.8 collective-permute-start.35
  943.8 9.0 collective-permute-start.36
  944.0 9.9 collective-permute-start.37
  953.8 9.0 collective-permute-start.38
  954.0 9.9 collective-permute-start.39
  963.8 9.0 collective-permute-start.40
  964.0 9.9 collective-permute-start.41
  973.8 9.3 collective-permute-start.42
  974.0 10.2 collective-permute-start.43
  984.1 8.9 collective-permute-start.44
  (6 other events, 51.1 us)
Sparse Core Ops, SparseCore 0:
  19.3 83.3 reduce-scatter.3
  110.9 122.9 all-reduce.6
  323.5 15.4 all-reduce.8
  353.2 81.7 reduce-scatter.5
  443.2 123.1 all-reduce.10
  665.3 15.4 all-reduce.12
  695.3 81.7 reduce-scatter.7
  785.4 123.1 all-reduce.14
  1006.6 15.4 all-reduce.16
